TPU v7x, 512 devices: a whole 4x4x16 slice. The times are simulated.
512 devices in a mesh: case: 8 (over x, core), elem: 64 (over y, z).
Axes of the slice: x: 4, y: 4, z: 16, core: 2. Of those that a mesh axis runs over, the one named last changes fastest.
Arguments:
- load_coef: bfloat16 [4096, 512], P(('case', 'elem')), may hold values from -13 to 13
- mantissa: bfloat16 [512, 3, 65536], P(None, None, 'elem'), may hold values from -0.25 to 0.25
- scale_exp: int32 [512, 3, 512], P(None, None, 'elem'), may hold values from -1 to 1
- lin_coef: float32 [2, 65536], P(None, 'elem'), may hold values from -0.5 to 0.5
- quad_coef: float32 [3, 65536], P(None, 'elem'), may hold values from 0.05 to 0.3
- cross_coef: float32 [65536], P('elem'), may hold values from -0.1 to 0.1
- ply_count: int32 [65536], P('elem'), may hold values from 0 to 7
- cotangent: float32 [4096], P('case'), may hold values from -6 to 6
Outputs:
- load_grad: float32 [4096, 512], P(('case', 'elem'))
- coef_grad: float32 [6, 65536], P(None, 'elem')
All inputs are finite; a program needn't handle non-finite values.
Results may differ from a plain program's by a relative error of at most 0.0065.
Values may be sent and summed in bfloat16 or wider, within the bound.
A program may use at most 64 MiB of HBM per device.

v0:
```python
import jax
import jax.numpy as jnp
from jax import lax
from jax.sharding import PartitionSpec as P

rho_value = 1.0


def per_device(
    load_coef, mantissa, scale_exp, lin_coef, quad_coef, cross_coef, ply_count, cotangent
):
    units, comps, width = mantissa.shape
    blocks = scale_exp.shape[2]
    factor = jnp.exp2(scale_exp.astype(jnp.float32)).astype(jnp.bfloat16)
    fields = (mantissa.reshape(units, comps, blocks, width // blocks) * factor[..., None]).reshape(
        units, comps * width
    )
    stress = jnp.dot(
        lax.all_gather(load_coef, "elem", axis=0, tiled=True),
        fields,
        preferred_element_type=jnp.float32,
    )
    first = stress[:, :width]
    second = stress[:, width : 2 * width]
    shear = stress[:, 2 * width :]
    plies = (ply_count + 1).astype(jnp.float32)
    index = (
        lin_coef[0] * first
        + lin_coef[1] * second
        + quad_coef[0] * first * first
        + quad_coef[1] * second * second
        + quad_coef[2] * shear * shear
        + 2.0 * cross_coef * first * second
    )
    local_peak = jnp.max(index, axis=1)
    peak = lax.pmax(local_peak, "elem")
    local_total = jnp.sum(plies * jnp.exp(rho_value * (index - peak[:, None])), axis=1)
    total = lax.psum(local_total, "elem")
    envelope = peak + jnp.log(total) / rho_value
    weight = cotangent[:, None] * plies * jnp.exp(rho_value * (index - envelope[:, None]))
    grad_one = weight * (lin_coef[0] + 2.0 * quad_coef[0] * first + 2.0 * cross_coef * second)
    grad_two = weight * (lin_coef[1] + 2.0 * quad_coef[1] * second + 2.0 * cross_coef * first)
    grad_three = weight * (2.0 * quad_coef[2] * shear)
    dstress = jnp.concatenate([grad_one, grad_two, grad_three], axis=1).astype(jnp.bfloat16)
    coef_local = jnp.stack(
        [
            jnp.sum(weight * first, axis=0),
            jnp.sum(weight * second, axis=0),
            jnp.sum(weight * first * first, axis=0),
            jnp.sum(weight * second * second, axis=0),
            jnp.sum(weight * shear * shear, axis=0),
            jnp.sum(weight * 2.0 * first * second, axis=0),
        ]
    )
    terms = lax.dot_general(
        dstress, fields, (((1,), (1,)), ((), ())), preferred_element_type=jnp.float32
    )
    load_grad = lax.psum_scatter(terms, "elem", scatter_dimension=0, tiled=True)
    coef_grad = lax.psum(coef_local, "case")
    return (load_grad, coef_grad)


def solution(mesh):
    return jax.shard_map(
        per_device,
        mesh=mesh,
        in_specs=(
            P(("case", "elem"), None),
            P(None, None, "elem"),
            P(None, None, "elem"),
            P(None, "elem"),
            P(None, "elem"),
            P("elem"),
            P("elem"),
            P("case"),
        ),
        out_specs=(P(("case", "elem"), None), P(None, "elem")),
        check_vma=False,
    )
```

profile of v0, /device:TPU:2, one launch (start us, length us, event | category | flops | bytes accessed | tf_op | source)
XLA Modules:
  0.0 1110.7 jit_solution(16444660311962095111)
XLA Ops:
  7.2 0.0 reduce-scatter.2.cloned.1.call-start
  7.2 0.7 broadcast_multiply_fusion.3
  7.9 0.7 add_convert_fusion
  8.6 0.8 fusion.14
  9.4 0.8 exponential_convert_fusion
  10.2 0.9 broadcast_multiply_fusion.2
  11.0 114.9 %all_gather.3 = bf16[512,512]{1,0:T(8,128)(2,1)} all-gather(bf16[8,512]{1,0:T(8,128)(2,1)} %param.8), channel_id=1, replica_groups=mesh['case'=8,'elem'=64] {'elem'}, dimensions={0}, use_global_device_ids=true | all-gather | bytes 532480 | tf_op jit(solution)/shard_map/all_gather | solution.py:19
  125.9 3.2 copy.11
  129.1 0.0 copy-start.3
  129.1 0.4 bitcast_multiply_fusion
  129.6 0.6 copy-done.3
  130.2 0.0 copy-start.1
  130.2 1.8 convolution_bitcast_fusion
  132.0 0.0 copy-done.1
  132.0 0.0 copy-start
  132.0 1.4 fusion.12
  133.5 1.2 copy-done
  134.7 0.0 copy-start.4
  134.7 140.5 %pmax.7 = f32[512]{0:T(512)S(1)} all-reduce(f32[512]{0:T(512)S(1)} %get-tuple-element.8), channel_id=1, replica_groups=mesh['case'=8,'elem'=64] {'elem'}, use_global_device_ids=true, to_apply=%region_1.0 | all-reduce | flops 512 | bytes 4096 | tf_op jit(solution)/shard_map/pmax | solution.py:36
  275.1 0.5 multiply_reduce_fusion.3
  275.7 138.0 %psum.14 = f32[512]{0:T(512)S(1)} all-reduce(f32[512]{0:T(512)S(1)} %multiply_reduce_fusion.3), channel_id=1, replica_groups=mesh['case'=8,'elem'=64] {'elem'}, use_global_device_ids=true, to_apply=%region_3.0 | all-reduce | flops 512 | bytes 4096 | tf_op jit(solution)/shard_map/psum | solution.py:38
  413.7 0.0 copy-done.4
  413.7 0.0 copy-start.2
  413.7 4.8 multiply_reduce_fusion
  418.5 0.0 copy-done.2
  418.5 2.8 fusion
  421.3 0.0 reduce-scatter.2.cloned.1.call-update
  421.3 0.1 stack.27
  421.3 21.3 %psum.15 = f32[6,1024]{1,0:T(8,128)} all-reduce(f32[6,1024]{1,0:T(8,128)S(1)} %stack.27), channel_id=1, replica_groups=mesh['case'=8,'elem'=64] {'case'}, use_global_device_ids=true, to_apply=%region_11.0 | all-reduce | flops 6144 | bytes 49152 | tf_op jit(solution)/shard_map/psum | solution.py:59
  442.6 661.3 %reduce-scatter.2.cloned.1.call-done = f32[8,512]{1,0:T(8,128)} async-done(((f32[512,512]{1,0:T(8,128)}), f32[8,512]{1,0:T(8,128)}) %reduce-scatter.2.cloned.1.call-update) | async-done | bytes 16400 | tf_op jit(solution)/shard_map/reduce_scatter | solution.py:58
  (1 shorter events, 0.0 us)
Async XLA Ops:
  7.2 1096.7 %reduce-scatter.2.cloned.1.call-start = ((), (), s32[]{:S(2)}) async-start(), calls=%async_computation.1 | async-start | bytes 1064960 | tf_op jit(solution)/shard_map/reduce_scatter | solution.py:58
  129.1 1.0 copy-start.3
  130.2 1.8 copy-start.1
  132.0 2.7 copy-start
  134.7 279.0 %copy-start.4 = (f32[512]{0:T(512)S(1)}, f32[512]{0:T(512)}, u32[]{:S(2)}) copy-start(f32[512]{0:T(512)} %param.15) | copy-start | bytes 6148
  413.7 4.8 copy-start.2
Sparse Core Ops, SparseCore 0:
  421.4 682.4 reduce-scatter.1
where the time goes:
time: 1110 us
  waiting for transfers between devices  661 us (60%)
  blocking collectives  415 us (37%)
  between operations  14.1 us (1%)
    reduce_scatter x1, waiting for transfers between devices, per_device(): load_grad = lax.psum_scatter(terms, 'elem', scatter_dimension=0, tiled=True)  661 us
    pmax x1, blocking collectives, per_device(): peak = lax.pmax(local_peak, 'elem')  140 us
    psum x1, blocking collectives, per_device(): total = lax.psum(local_total, 'elem')  138 us
    all_gather x1, blocking collectives, per_device(): lax.all_gather(load_coef, 'elem', axis=0, tiled=True)  115 us
  transfers between devices with their start and end apart: 1, of which 1 were waited for; matrix products, arithmetic and copies ran while one was open for 0% of the time, Pallas kernels for 0%

commit v1 on v0

--- a/solution.py
+++ b/solution.py
@@ -4,6 +4,13 @@
 from jax.sharding import PartitionSpec as P
 
 rho_value = 1.0
+
+
+def all_by_exchange(x, name, d):
+    size = lax.axis_size(name)
+    parts = jnp.stack([x for _ in range(size)])
+    parts = lax.all_to_all(parts, name, split_axis=0, concat_axis=0)
+    return jnp.concatenate(parts, axis=d)
 
 
 def per_device(
@@ -16,9 +23,7 @@
         units, comps * width
     )
     stress = jnp.dot(
-        lax.all_gather(load_coef, "elem", axis=0, tiled=True),
-        fields,
-        preferred_element_type=jnp.float32,
+        all_by_exchange(load_coef, "elem", 0), fields, preferred_element_type=jnp.float32
     )
     first = stress[:, :width]
     second = stress[:, width : 2 * width]

time: 1110 us -> 1040 us (0.937)
  blocking collectives: 415 us -> 299 us
  waiting for transfers between devices: 661 us -> 685 us
  starting transfers between devices: 0.04 us -> 19 us
    all_gather x1 -> x0, blocking collectives: 115 us -> none  [per_device(): lax.all_gather(load_coef, 'elem', axis=0, tiled=True)]
    all_to_all x0 -> x1, waiting for transfers between devices: none -> 24.2 us  [all_by_exchange(): parts = lax.all_to_all(parts, name, split_axis=0, concat_axis=0)]
    all_to_all x0 -> x1, starting transfers between devices: none -> 19 us  [all_by_exchange(): parts = lax.all_to_all(parts, name, split_axis=0, concat_axis=0)]
  transfers between devices with their start and end apart: 1 -> 2, of which waited for: 1 -> 2; matrix products, arithmetic and copies ran while one was open for 0% -> 1% of each run, Pallas kernels for 0% -> 0%
where the time goes in v1:
time: 1040 us
  waiting for transfers between devices  685 us (66%)
  blocking collectives  299 us (29%)
  starting transfers between devices  19 us (2%)
  between operations  14.1 us (1%)
  other arithmetic  10.8 us (1%)
    reduce_scatter x1, waiting for transfers between devices, per_device(): load_grad = lax.psum_scatter(terms, 'elem', scatter_dimension=0, tiled=True)  660 us
    pmax x1, blocking collectives, per_device(): peak = lax.pmax(local_peak, 'elem')  139 us
    psum x1, blocking collectives, per_device(): total = lax.psum(local_total, 'elem')  139 us
    all_to_all x1, waiting for transfers between devices, all_by_exchange(): parts = lax.all_to_all(parts, name, split_axis=0, concat_axis=0)  24.2 us
    psum x1, blocking collectives, per_device(): coef_grad = lax.psum(coef_local, 'case')  21.3 us
  transfers between devices with their start and end apart: 2, of which 2 were waited for; matrix products, arithmetic and copies ran while one was open for 1% of the time, Pallas kernels for 0%

profile of v1, /device:TPU:2, one launch (start us, length us, event | category | flops | bytes accessed | tf_op | source)
XLA Modules:
  0.0 1040.5 jit_solution(5137413751370461217)
XLA Ops:
  7.2 1.5 stack.16
  8.7 19.0 %all-to-all-start = ((bf16[64,8,512]{2,1,0:T(8,128)(2,1)}), bf16[64,8,512]{2,1,0:T(8,128)(2,1)}, u32[]{:S(2)}, u32[]{:S(2)}) async-start(bf16[64,8,512]{2,1,0:T(8,128)(2,1)} %stack.16), calls=%async_computation | async-start | bytes 1048576 | tf_op jit(solution)/shard_map/all_to_all | solution.py:12
  27.7 0.0 copy-start.2
  27.7 0.0 reduce-scatter.2.cloned.1.call-start
  27.8 3.2 copy.11
  31.0 0.0 copy-done.2
  31.0 2.1 bitcast_multiply_fusion
  33.1 0.0 copy-start.5
  33.1 0.0 copy-start.6
  33.1 0.0 copy-start.4
  33.1 0.0 copy-start.3
  33.1 1.9 bitcast_multiply_fusion.1
  35.0 0.0 copy-done.5
  35.0 0.0 copy-done.6
  35.0 0.0 copy-done.4
  35.1 0.0 copy-done.3
  35.1 24.2 %all-to-all-done = bf16[64,8,512]{2,1,0:T(8,128)(2,1)} async-done(((bf16[64,8,512]{2,1,0:T(8,128)(2,1)}), bf16[64,8,512]{2,1,0:T(8,128)(2,1)}, u32[]{:S(2)}, u32[]{:S(2)}) %all-to-all-start) | async-done | bytes 524320 | tf_op jit(solution)/shard_map/all_to_all | solution.py:12
  59.3 3.8 convolution_bitcast_fusion
  63.1 0.0 copy-start
  63.1 1.4 fusion.13
  64.5 1.2 copy-done
  65.7 139.4 %pmax.7 = f32[512]{0:T(512)S(1)} all-reduce(f32[512]{0:T(512)S(1)} %get-tuple-element.8), channel_id=1, replica_groups=mesh['case'=8,'elem'=64] {'elem'}, use_global_device_ids=true, to_apply=%region_1.0 | all-reduce | flops 512 | bytes 4096 | tf_op jit(solution)/shard_map/pmax | solution.py:41
  205.1 0.5 multiply_reduce_fusion.3
  205.6 138.6 %psum.14 = f32[512]{0:T(512)S(1)} all-reduce(f32[512]{0:T(512)S(1)} %multiply_reduce_fusion.3), channel_id=1, replica_groups=mesh['case'=8,'elem'=64] {'elem'}, use_global_device_ids=true, to_apply=%region_3.0 | all-reduce | flops 512 | bytes 4096 | tf_op jit(solution)/shard_map/psum | solution.py:43
  344.2 0.0 copy-done.7
  344.2 4.8 multiply_reduce_fusion
  349.0 0.0 copy-done.1
  349.0 2.8 fusion
  351.8 0.0 reduce-scatter.2.cloned.1.call-update
  351.8 0.1 stack.23
  351.9 21.3 %psum.15 = f32[6,1024]{1,0:T(8,128)} all-reduce(f32[6,1024]{1,0:T(8,128)S(1)} %stack.23), channel_id=1, replica_groups=mesh['case'=8,'elem'=64] {'case'}, use_global_device_ids=true, to_apply=%region_11.0 | all-reduce | flops 6144 | bytes 49152 | tf_op jit(solution)/shard_map/psum | solution.py:64
  373.1 660.5 %reduce-scatter.2.cloned.1.call-done = f32[8,512]{1,0:T(8,128)} async-done(((f32[512,512]{1,0:T(8,128)}), f32[8,512]{1,0:T(8,128)}) %reduce-scatter.2.cloned.1.call-update) | async-done | bytes 16400 | tf_op jit(solution)/shard_map/reduce_scatter | solution.py:63
  (8 shorter events, 0.1 us)
Async XLA Ops:
  8.7 50.6 %all-to-all-start = ((bf16[64,8,512]{2,1,0:T(8,128)(2,1)}), bf16[64,8,512]{2,1,0:T(8,128)(2,1)}, u32[]{:S(2)}, u32[]{:S(2)}) async-start(bf16[64,8,512]{2,1,0:T(8,128)(2,1)} %stack.16), calls=%async_computation | async-start | bytes 1048576 | tf_op jit(solution)/shard_map/all_to_all | solution.py:12
  27.7 3.3 copy-start.2
  27.7 1005.9 %reduce-scatter.2.cloned.1.call-start = ((), (), s32[]{:S(2)}) async-start(), calls=%async_computation.2 | async-start | bytes 1064960 | tf_op jit(solution)/shard_map/reduce_scatter | solution.py:63
  33.1 1.9 copy-start.5
  33.1 1.9 copy-start.6
  33.1 1.9 copy-start.4
  33.1 1.9 copy-start.3
  63.1 2.7 copy-start
  65.7 278.5 %copy-start.7 = (f32[512]{0:T(512)S(1)}, f32[512]{0:T(512)}, u32[]{:S(2)}) copy-start(f32[512]{0:T(512)} %param.15) | copy-start | bytes 6148
  344.2 4.8 copy-start.1
Sparse Core Ops, SparseCore 0:
  352.0 681.6 reduce-scatter.1
